TPU v7x, 32 devices: a whole 2x2x4 slice. The times are simulated.
32 devices in a mesh: lat: 16 (over z, x, core), wid: 2 (over y).
Axes of the slice: x: 2, y: 2, z: 4, core: 2. Of those that a mesh axis runs over, the one named last changes fastest.
Arguments:
- buffer_src: bfloat16 [1728, 3584], P('lat', 'wid'), may hold values from -6 to 6
- buffer_tgt: bfloat16 [1728, 3, 3584], P('lat', None, 'wid'), may hold values from -6 to 6
- batch_rows: int32 [1536], replicated, may hold values from 0 to 1727, as said below
- enc_w: float32 [3584, 8192], P('wid', 'lat'), may hold values from -0.09375 to 0.09375
- enc_b: float32 [8192], P('lat'), may hold values from -3 to 3
- dec_w: float32 [3, 8192, 3584], P(None, 'lat', 'wid'), may hold values from -0.0625 to 0.0625
- dec_b: float32 [3, 3584], P(None, 'wid'), may hold values from -3 to 3
- enc_m: float32 [3584, 8192], P('wid', 'lat'), may hold values from -40 to 40
- enc_v: float32 [3584, 8192], P('wid', 'lat'), may hold values from 3 to 300
- dec_m: float32 [3, 8192, 3584], P(None, 'lat', 'wid'), may hold values from -20 to 20
- dec_v: float32 [3, 8192, 3584], P(None, 'lat', 'wid'), may hold values from 3 to 300
Outputs:
- enc_w_new: float32 [3584, 8192], P('wid', 'lat')
- enc_m_new: float32 [3584, 8192], P('wid', 'lat')
- enc_v_new: float32 [3584, 8192], P('wid', 'lat')
- dec_w_new: float32 [3, 8192, 3584], P(None, 'lat', 'wid')
- dec_m_new: float32 [3, 8192, 3584], P(None, 'lat', 'wid')
- dec_v_new: float32 [3, 8192, 3584], P(None, 'lat', 'wid')
Inputs may be any that keep to these rules, and one draw needn't show every extreme that they name: `batch_rows`: 1536 different rows of the buffer.
All inputs are finite; a program needn't handle non-finite values.
Results may differ from a plain program's by a relative error of at most 0.0035.
Values may be sent and summed in bfloat16 or wider, within the bound.
A program may use at most 256 MiB of HBM per device.

v0:
```python
import jax
import jax.numpy as jnp
from jax import lax
from jax.sharding import PartitionSpec as P

STEP = 100


def smooth(pre):
    return jax.nn.softplus(4.0 * pre) * 0.25


def adam(weight, grad, first, second):
    first_new = 0.9 * first + 0.1 * grad
    second_new = 0.999 * second + 0.001 * grad * grad
    fix_one = 1.0 - 0.9**STEP
    fix_two = 1.0 - 0.999**STEP
    weight_new = weight - 0.001 * (first_new / fix_one) / (jnp.sqrt(second_new / fix_two) + 1e-08)
    return (weight_new, first_new, second_new)


def on_device(
    buffer_src, buffer_tgt, batch_rows, enc_w, enc_b, dec_w, dec_b, enc_m, enc_v, dec_m, dec_v
):
    lat_count = lax.axis_size("lat")
    lat_place = lax.axis_index("lat")
    tokens = batch_rows.shape[0]
    share = tokens // lat_count
    every_src = lax.all_gather(buffer_src, "lat", axis=0, tiled=True)
    source = jnp.take(every_src, batch_rows, axis=0)
    enc_half = enc_w.astype(jnp.bfloat16)
    dec_half = dec_w.astype(jnp.bfloat16)
    partial_pre = jnp.dot(source, enc_half, preferred_element_type=jnp.float32)
    pre = lax.psum(partial_pre, "wid") + enc_b
    act = smooth(pre).astype(jnp.bfloat16)
    slope = jax.nn.sigmoid(4.0 * pre)
    pred = lax.psum_scatter(
        jnp.einsum("tl,kld->tkd", act, dec_half, preferred_element_type=jnp.float32),
        "lat",
        scatter_dimension=0,
        tiled=True,
    )
    every_tgt = lax.all_gather(buffer_tgt, "lat", axis=0, tiled=True)
    mine = lax.dynamic_slice_in_dim(batch_rows, lat_place * share, share, 0)
    target = jnp.take(every_tgt, mine, axis=0)
    err_mine = (pred + dec_b[None] - target.astype(jnp.float32)).astype(jnp.bfloat16)
    err_all = lax.all_gather(err_mine, "lat", axis=0, tiled=True)
    grad_dec = jnp.einsum("tl,tkd->kld", act, err_all, preferred_element_type=jnp.float32)
    partial_back = jnp.einsum("tkd,kld->tl", err_all, dec_half, preferred_element_type=jnp.float32)
    grad_act = lax.psum(partial_back, "wid")
    grad_pre = (grad_act * slope).astype(jnp.bfloat16)
    grad_enc = jnp.einsum("td,tl->dl", source, grad_pre, preferred_element_type=jnp.float32)
    enc_w_new, enc_m_new, enc_v_new = adam(enc_w, grad_enc, enc_m, enc_v)
    dec_w_new, dec_m_new, dec_v_new = adam(dec_w, grad_dec, dec_m, dec_v)
    return (enc_w_new, enc_m_new, enc_v_new, dec_w_new, dec_m_new, dec_v_new)


def solution(mesh):
    placed = (
        P("lat", "wid"),
        P("lat", None, "wid"),
        P(),
        P("wid", "lat"),
        P("lat"),
        P(None, "lat", "wid"),
        P(None, "wid"),
        P("wid", "lat"),
        P("wid", "lat"),
        P(None, "lat", "wid"),
        P(None, "lat", "wid"),
    )
    return jax.shard_map(
        on_device,
        mesh=mesh,
        in_specs=placed,
        out_specs=(
            P("wid", "lat"),
            P("wid", "lat"),
            P("wid", "lat"),
            P(None, "lat", "wid"),
            P(None, "lat", "wid"),
            P(None, "lat", "wid"),
        ),
        check_vma=False,
    )
```

profile of v0, /device:TPU:0, one launch (start us, length us, event | category | flops | bytes accessed | tf_op | source)
XLA Modules:
  0.0 903.2 jit_solution(4185787774456620320)
XLA Ops:
  7.2 0.7 all-gather.9.cloned.1.call-update
  7.9 0.0 all-reduce.3.cloned.1.call-start
  7.9 0.7 compare_select_fusion.1
  8.7 0.7 compare_and_fusion
  9.4 65.7 %all-gather.9.cloned.1.call-done = bf16[16,108,1792]{2,1,0:T(8,128)(2,1)} async-done(((bf16[1,108,1792]{2,1,0:T(8,128)(2,1)}), bf16[16,108,1792]{2,1,0:T(8,128)(2,1)}) %all-gather.9.cloned.1.call-update) | async-done | bytes 6193168 | tf_op jit(solution)/shard_map/all_gather | solution.py:29
  75.1 8.2 reshape.43
  83.2 14.9 %gather_fusion = bf16[1536,1792]{1,0:T(8,128)(2,1)} fusion(bf16[1728,1792]{1,0:T(8,128)(2,1)} %reshape.43, s32[2048]{0:T(1024)S(1)} %pad_clamp_fusion), kind=kCustom, calls=%fused_computation | custom fusion | bytes 11016192 | tf_op jit(solution)/shard_map/jit(_take)/gather | solution.py:30
  98.2 8.4 fusion.9
  106.6 0.0 all-gather.5.cloned.1.call-start
  106.7 1.2 copy-done
  107.9 1.9 copy.31
  109.8 0.0 reduce-scatter.2.cloned.1.call-start
  109.9 81.4 %all-reduce.3.cloned.1.call-done = f32[1536,512]{1,0:T(8,128)} async-done(((f32[1536,512]{1,0:T(8,128)}), f32[1536,512]{1,0:T(8,128)}) %all-reduce.3.cloned.1.call-update) | async-done | bytes 3145744 | tf_op jit(solution)/shard_map/psum | solution.py:34
  191.3 21.0 %fusion.6 = f32[1536,3,1792]{2,0,1:T(8,128)} fusion(f32[3,512,1792]{2,1,0:T(8,128)} %param.16, f32[1536,512]{1,0:T(8,128)} %all-reduce.3.cloned.1.call-done, f32[512]{0:T(512)S(1)} %copy-done.2), kind=kOutput, calls=%fused_computation.19 | convolution fusion | flops 8466333696 | bytes 47187968 | tf_op jit(solution)/shard_map/tl,kld->tkd/dot_general | solution.py:38
  212.4 0.2 all-gather.7.cloned.1.call-start
  212.6 0.8 compare_and_fusion.1
  213.4 106.8 %all-gather.5.cloned.1.call-done = bf16[1728,3,1792]{2,1,0:T(4,128)(2,1)} async-done(((bf16[108,3,1792]{2,1,0:T(4,128)(2,1)}), bf16[1728,3,1792]{2,1,0:T(4,128)(2,1)}) %all-gather.5.cloned.1.call-update) | async-done | bytes 18579472 | tf_op jit(solution)/shard_map/all_gather | solution.py:43
  320.2 9.8 %gather_fusion.1 = bf16[96,3,1792]{2,1,0:T(4,128)(2,1)S(1)} fusion(bf16[1728,3,1792]{2,1,0:T(4,128)(2,1)} %all-gather.5.cloned.1.call-done, s32[1024]{0:T(1024)S(1)} %pad_clamp_fusion.1), kind=kCustom, calls=%fused_computation.1 | custom fusion | bytes 2064768 | tf_op jit(solution)/shard_map/jit(_take)/gather | solution.py:45
  330.0 321.5 %reduce-scatter.2.cloned.1.call-done = f32[96,3,1792]{2,0,1:T(8,128)} async-done(((f32[1536,3,1792]{2,0,1:T(8,128)}), f32[96,3,1792]{2,0,1:T(8,128)}) %reduce-scatter.2.cloned.1.call-update) | async-done | bytes 2064400 | tf_op jit(solution)/shard_map/reduce_scatter | solution.py:37
  651.5 2.9 subtract_convert_fusion
  654.5 0.0 all-reduce.5.cloned.1.call-start
  654.5 12.3 %copy.35 = f32[3,512,1792]{1,2,0:T(8,128)} copy(f32[3,512,1792]{2,1,0:T(8,128)} %param.16) | data formatting | bytes 22020096 | tf_op args[5]
  666.8 12.1 %copy.33 = f32[3,512,1792]{1,2,0:T(8,128)} copy(f32[3,512,1792]{2,1,0:T(8,128)} %param.20) | data formatting | bytes 22020096 | tf_op args[9]
  678.9 12.1 %copy.34 = f32[3,512,1792]{1,2,0:T(8,128)} copy(f32[3,512,1792]{2,1,0:T(8,128)} %param.21) | data formatting | bytes 22020096 | tf_op args[10]
  691.0 87.5 %all-gather.7.cloned.1.call-done = bf16[1536,3,1792]{2,0,1:T(8,128)(2,1)} async-done(((bf16[96,3,1792]{2,0,1:T(8,128)(2,1)}), bf16[1536,3,1792]{2,0,1:T(8,128)(2,1)}) %all-gather.7.cloned.1.call-update) | async-done | bytes 16515088 | tf_op jit(solution)/shard_map/all_gather | solution.py:47
  778.5 16.6 %convolution_bitcast_fusion = f32[1536,512]{1,0:T(8,128)} fusion(bf16[1536,3,1792]{2,0,1:T(8,128)(2,1)} %all-gather.7.cloned.1.call-done, f32[3,512,1792]{2,1,0:T(8,128)} %param.16), kind=kOutput, calls=%fused_computation.13 | convolution fusion | flops 8458469376 | bytes 30670848 | tf_op jit(solution)/shard_map/tkd,kld->tl/dot_general | solution.py:49
  795.1 39.0 %divide_subtract_fusion = (f32[3,512,1792]{1,2,0:T(8,128)}, f32[3,512,1792]{1,2,0:T(8,128)}, f32[3,512,1792]{1,2,0:T(8,128)}) fusion(f32[3,512,1792]{1,2,0:T(8,128)} %copy.35, f32[3,512,1792]{1,2,0:T(8,128)} %copy.33, f32[3,512,1792]{1,2,0:T(8,128)} %copy.34, bf16[1536,3,1792]{2,0,1:T(8,128)(2,1)} %all-gather.7.cloned.1.call-done, ...), kind=kOutput, calls=%fused_computation.6 | convolution fusion | flops 8496611328 | bytes 85723136 | tf_op jit(solution)/shard_map/tl,tkd->kld/dot_general | solution.py:48
  834.1 12.3 %copy.36 = f32[3,512,1792]{2,1,0:T(8,128)} copy(f32[3,512,1792]{1,2,0:T(8,128)} %get-tuple-element.24) | data formatting | bytes 22020096
  846.4 12.1 %copy.37 = f32[3,512,1792]{2,1,0:T(8,128)} copy(f32[3,512,1792]{1,2,0:T(8,128)} %get-tuple-element.25) | data formatting | bytes 22020096
  858.6 12.1 %copy.38 = f32[3,512,1792]{2,1,0:T(8,128)} copy(f32[3,512,1792]{1,2,0:T(8,128)} %get-tuple-element.26) | data formatting | bytes 22020096
  870.7 8.5 all-reduce.5.cloned.1.call-done
  879.1 17.2 %divide_subtract_fusion.1 = (f32[1792,512]{1,0:T(8,128)}, f32[1792,512]{1,0:T(8,128)}, f32[1792,512]{1,0:T(8,128)}) fusion(f32[1792,512]{1,0:T(8,128)} %param.14, f32[1792,512]{1,0:T(8,128)} %param.18, f32[1792,512]{1,0:T(8,128)} %param.19, f32[1536,512]{1,0:T(8,128)} %all-reduce.5.cloned.1.call-done, f32[1536,512]{1,0:T(8,128)} %all-reduce.3.cloned.1.call-done, ...), kind=kOutput, calls=%fused_computation.11 | convolution fusion | flops 2837839872 | bytes 33820160 | tf_op jit(solution)/shard_map/td,tl->dl/dot_general | solution.py:52
  (13 shorter events, 0.1 us)
Async XLA Ops:
  7.2 67.9 %all-gather.9.cloned.1.call-start = ((), (), s32[]{:S(2)}) async-start(), calls=%async_computation.6 | async-start | bytes 6823936 | tf_op jit(solution)/shard_map/all_gather | solution.py:29
  7.9 183.4 %all-reduce.3.cloned.1.call-start = ((), (), s32[]{:S(2)}) async-start(), calls=%async_computation.1 | async-start | bytes 6291456 | tf_op jit(solution)/shard_map/psum | solution.py:34
  106.6 1.3 copy-start
  106.6 84.7 %copy-start.2 = (f32[512]{0:T(512)S(1)}, f32[512]{0:T(512)}, u32[]{:S(2)}) copy-start(f32[512]{0:T(512)} %param.15) | copy-start | bytes 6148
  106.6 213.6 %all-gather.5.cloned.1.call-start = ((), (), s32[]{:S(2)}) async-start(), calls=%async_computation.3 | async-start | bytes 26320896 | tf_op jit(solution)/shard_map/all_gather | solution.py:43
  109.8 541.7 %reduce-scatter.2.cloned.1.call-start = ((), (), s32[]{:S(2)}) async-start(), calls=%async_computation.2 | async-start | bytes 35094528 | tf_op jit(solution)/shard_map/reduce_scatter | solution.py:37
  212.4 439.2 %copy-start.1 = (f32[3,1792]{1,0:T(4,128)S(1)}, f32[3,1792]{1,0:T(4,128)}, u32[]{:S(2)}) copy-start(f32[3,1792]{1,0:T(4,128)} %param.17) | copy-start | bytes 64516
  212.4 566.1 %all-gather.7.cloned.1.call-start = ((), (), s32[]{:S(2)}) async-start(), calls=%async_computation.4 | async-start | bytes 17547264 | tf_op jit(solution)/shard_map/all_gather | solution.py:47
  654.5 224.7 %all-reduce.5.cloned.1.call-start = ((), (), s32[]{:S(2)}) async-start(), calls=%async_computation.5 | async-start | bytes 6291456 | tf_op jit(solution)/shard_map/psum | solution.py:50
Sparse Core Ops, SparseCore 0:
  10.3 64.7 all-gather.8
  106.7 84.5 all-reduce.2
  193.5 126.6 all-gather.4
  324.4 327.0 reduce-scatter.1
  654.6 123.8 all-gather.6
  795.2 83.8 all-reduce.4
where the time goes:
time: 905 us; the launch traced here: 903 us
  waiting for transfers between devices  672 us (74%)
  local copies, waits for them, and re-layouts  109 us (12%)
  matrix products  102 us (11%)
  between operations  14.1 us (2%)
    reduce_scatter x1, waiting for transfers between devices, on_device(): lax.psum_scatter(jnp.einsum('tl,kld->tkd', act, dec_half, preferred_eleme...  322 us
    all_gather x1, waiting for transfers between devices, on_device(): every_tgt = lax.all_gather(buffer_tgt, 'lat', axis=0, tiled=True)  107 us
    all_gather x1, waiting for transfers between devices, on_device(): err_all = lax.all_gather(err_mine, 'lat', axis=0, tiled=True)  87.5 us
    unnamed x14, local copies, waits for them, and re-layouts  84.4 us
    psum x1, waiting for transfers between devices, on_device(): pre = lax.psum(partial_pre, 'wid') + enc_b  81.4 us
    all_gather x1, waiting for transfers between devices, on_device(): every_src = lax.all_gather(buffer_src, 'lat', axis=0, tiled=True)  65.7 us
    dot_general x1, matrix products, on_device(): jnp.einsum('tl,tkd->kld', act, err_all, preferred_element_type=jnp.float32)  39 us
    dot_general x1, matrix products, on_device(): jnp.einsum('tl,kld->tkd', act, dec_half, preferred_element_type=jnp.float32)  21 us
  transfers between devices with their start and end apart: 6, of which 6 were waited for; matrix products, arithmetic and copies ran while one was open for 16% of the time, Pallas kernels for 0%

commit v1 on v0

v1 whole, which is shorter than its diff:
```python
import functools

import jax
import jax.numpy as jnp
from jax import lax
from jax.experimental import pallas as pl
from jax.experimental.pallas import tpu as pltpu
from jax.sharding import PartitionSpec as P

STEP = 100
FIX_ONE = 1.0 - 0.9**STEP
FIX_TWO = 1.0 - 0.999**STEP
VMEM_LIMIT = 48 * 1024 * 1024


def adam_into(grad, w_ref, m_ref, v_ref, w_out, m_out, v_out):
    first_new = 0.9 * m_ref[...] + 0.1 * grad
    second_new = 0.999 * v_ref[...] + 0.001 * grad * grad
    m_out[...] = first_new
    v_out[...] = second_new
    w_out[...] = w_ref[...] - 0.001 * (first_new * (1.0 / FIX_ONE)) / (
        jnp.sqrt(second_new * (1.0 / FIX_TWO)) + 1e-08
    )


def over_tokens(a, b):
    return lax.dot_general(a, b, (((0,), (0,)), ((), ())), preferred_element_type=jnp.float32)


def dec_kernel(act_a, act_b, err_a, err_b, w_ref, m_ref, v_ref, *rest):
    w_out, m_out, v_out = rest[-3:]
    grad = jnp.dot(act_a[...], err_a[...], preferred_element_type=jnp.float32)
    grad = grad + jnp.dot(act_b[...], err_b[...], preferred_element_type=jnp.float32)
    adam_into(grad, w_ref, m_ref, v_ref, w_out, m_out, v_out)


def dec_update(layer, act_ts, errs, dec_w, dec_m, dec_v, before):
    layers, lats, width = dec_w.shape
    block = 256 if width % 256 == 0 else 128
    whole = [pl.BlockSpec(a.shape, lambda j: (0, 0)) for a in act_ts]
    cols = [pl.BlockSpec((e.shape[0], block), lambda j: (0, j)) for e in errs]
    tile = pl.BlockSpec((None, lats, block), lambda j: (layer, 0, j))
    held = [pl.BlockSpec(memory_space=pl.ANY)] * len(before)
    tokens = sum(e.shape[0] for e in errs)
    return pl.pallas_call(
        dec_kernel,
        grid=(width // block,),
        in_specs=whole + cols + [tile] * 3 + held,
        out_specs=[tile] * 3,
        out_shape=[jax.ShapeDtypeStruct(dec_w.shape, jnp.float32)] * 3,
        input_output_aliases={7 + i: i for i in range(len(before))},
        compiler_params=pltpu.CompilerParams(vmem_limit_bytes=VMEM_LIMIT),
        cost_estimate=pl.CostEstimate(
            flops=2 * tokens * lats * width,
            bytes_accessed=24 * lats * width + 2 * tokens * width,
            transcendentals=lats * width,
        ),
        name="dec_update",
    )(*act_ts, *errs, dec_w, dec_m, dec_v, *before)


def enc_kernel(src_a, src_b, gp_a, gp_b, w_ref, m_ref, v_ref, w_out, m_out, v_out):
    grad = over_tokens(src_a[...], gp_a[...]) + over_tokens(src_b[...], gp_b[...])
    adam_into(grad, w_ref, m_ref, v_ref, w_out, m_out, v_out)


def enc_update(srcs, gps, enc_w, enc_m, enc_v):
    width, lats = enc_w.shape
    block = 256 if width % 256 == 0 else 128
    whole = [pl.BlockSpec(g.shape, lambda j: (0, 0)) for g in gps]
    cols = [pl.BlockSpec((s.shape[0], block), lambda j: (0, j)) for s in srcs]
    tile = pl.BlockSpec((block, lats), lambda j: (j, 0))
    return pl.pallas_call(
        enc_kernel,
        grid=(width // block,),
        in_specs=cols + whole + [tile] * 3,
        out_specs=[tile] * 3,
        out_shape=[jax.ShapeDtypeStruct(enc_w.shape, jnp.float32)] * 3,
        compiler_params=pltpu.CompilerParams(vmem_limit_bytes=VMEM_LIMIT),
        name="enc_update",
    )(*srcs, *gps, enc_w, enc_m, enc_v)


def on_device(
    buffer_src, buffer_tgt, batch_rows, enc_w, enc_b, dec_w, dec_b, enc_m, enc_v, dec_m, dec_v
):
    lat_count = lax.axis_size("lat")
    wid_count = lax.axis_size("wid")
    lat_place = lax.axis_index("lat")
    core = lat_place % 2
    rows = buffer_src.shape[0]
    share = -(-rows // 16) * 16
    extra = share - rows
    layers = dec_w.shape[0]
    bf16 = jnp.bfloat16
    alike = [list(range(c, lat_count, 2)) for c in range(2)]
    partner = [(i, i ^ 1) for i in range(lat_count)]

    def swap(x):
        return lax.ppermute(x, "lat", partner)

    def across(x):
        low = x.astype(bf16)
        total = x
        for hop in range(1, wid_count):
            ring = [(i, (i + hop) % wid_count) for i in range(wid_count)]
            total = total + lax.ppermute(low, "wid", ring).astype(jnp.float32)
        return total

    def gather(x):
        mine = lax.all_gather(x, "lat", axis=0, tiled=True, axis_index_groups=alike)
        return mine, swap(mine)

    own = lat_place * rows + jnp.arange(rows, dtype=batch_rows.dtype)
    chosen = jnp.any(own[:, None] == batch_rows[None, :], axis=1)
    chosen = jnp.pad(chosen, (0, extra))[:, None]
    target = jnp.pad(buffer_tgt, ((0, extra), (0, 0), (0, 0)))

    srcs = gather(jnp.pad(buffer_src, ((0, extra), (0, 0))))
    enc_half = enc_w.astype(bf16)
    dec_half = [dec_w[k].astype(bf16) for k in range(layers)]
    acts, slopes = [], []
    for src in srcs:
        pre = across(jnp.dot(src, enc_half, preferred_element_type=jnp.float32)) + enc_b
        acts.append((jax.nn.softplus(4.0 * pre) * 0.25).astype(bf16))
        slopes.append(jax.nn.sigmoid(4.0 * pre))
    act_ts = [a.T for a in acts]

    errs = []
    for k in range(layers):
        theirs = jnp.dot(acts[1], dec_half[k], preferred_element_type=jnp.float32).astype(bf16)
        mine = jnp.dot(acts[0], dec_half[k], preferred_element_type=jnp.float32)
        both = (mine + swap(theirs).astype(jnp.float32)).astype(bf16)
        pred = lax.psum_scatter(
            both, "lat", scatter_dimension=0, tiled=True, axis_index_groups=alike
        )
        err = pred.astype(jnp.float32) + dec_b[k][None] - target[:, k].astype(jnp.float32)
        errs.append(gather(jnp.where(chosen, err, 0.0).astype(bf16)))

    dec_new = ()
    for k in range(layers):
        dec_new = dec_update(k, act_ts, errs[k], dec_w, dec_m, dec_v, dec_new)

    gps = []
    for half in range(2):
        back = sum(
            lax.dot_general(
                errs[k][half],
                dec_half[k],
                (((1,), (1,)), ((), ())),
                preferred_element_type=jnp.float32,
            )
            for k in range(layers)
        )
        gps.append((across(back) * slopes[half]).astype(bf16))
    enc_new = enc_update(srcs, gps, enc_w, enc_m, enc_v)
    return (*enc_new, *dec_new)


def solution(mesh):
    placed = (
        P("lat", "wid"),
        P("lat", None, "wid"),
        P(),
        P("wid", "lat"),
        P("lat"),
        P(None, "lat", "wid"),
        P(None, "wid"),
        P("wid", "lat"),
        P("wid", "lat"),
        P(None, "lat", "wid"),
        P(None, "lat", "wid"),
    )
    return jax.shard_map(
        on_device,
        mesh=mesh,
        in_specs=placed,
        out_specs=(
            P("wid", "lat"),
            P("wid", "lat"),
            P("wid", "lat"),
            P(None, "lat", "wid"),
            P(None, "lat", "wid"),
            P(None, "lat", "wid"),
        ),
        check_vma=False,
    )
```

time: 905 us -> 658 us (0.73)
  waiting for transfers between devices: 672 us -> 503 us
  local copies, waits for them, and re-layouts: 109 us -> 7.61 us
  Pallas kernels: 0 us -> 56.2 us
  matrix products: 102 us -> 56.4 us
  other arithmetic: 5.13 us -> 14.3 us
    reduce_scatter x1 -> x3, waiting for transfers between devices: 322 us -> 203 us  [on_device(): lax.psum_scatter(both, 'lat', scatter_dimension=0, tiled=True, axis_index...]
    psum x2 -> x0, waiting for transfers between devices: 89.9 us -> none  [the longest x1 81.4 us: on_device(): pre = lax.psum(partial_pre, 'wid') + enc_b]
    unnamed x14 -> x54, local copies, waits for them, and re-layouts: 84.4 us -> 4.71 us
    pallas_call x0 -> x4, Pallas kernels: none -> 56.2 us  [the longest x3 42.8 us: dec_update(): pl.pallas_call(dec_kernel, grid=(width // block,), in_specs=whole + cols...]
    ppermute x0 -> x11, waiting for transfers between devices: none -> 50.9 us  [the longest x4 33.9 us: across(): total = total + lax.ppermute(low, 'wid', ring).astype(jnp.float32)]
    dot_general x5 -> x14, matrix products: 102 us -> 56.4 us  [the longest x6 23.7 us: on_device(): lax.dot_general(errs[k][half], dec_half[k], (((1,), (1,)), ((), ())), pre...]
    gather x2 -> x0, local copies, waits for them, and re-layouts: 24.7 us -> none  [the longest x1 14.9 us: on_device(): source = jnp.take(every_src, batch_rows, axis=0)]
    all_gather x3 -> x4, waiting for transfers between devices: 260 us -> 248 us  [gather(): mine = lax.all_gather(x, 'lat', axis=0, tiled=True, axis_index_groups=alike)]
  transfers between devices with their start and end apart: 6 -> 18, of which waited for: 6 -> 12; matrix products, arithmetic and copies ran while one was open for 16% -> 8% of each run, Pallas kernels for 0% -> 7%
where the time goes in v1:
time: 658 us; the launch traced here: 657 us
  waiting for transfers between devices  503 us (76%)
  matrix products  56.4 us (9%)
  Pallas kernels  56.2 us (9%)
  between operations  14.5 us (2%)
  other arithmetic  14.3 us (2%)
  local copies, waits for them, and re-layouts  7.61 us (1%)
    all_gather x4, waiting for transfers between devices, gather(): mine = lax.all_gather(x, 'lat', axis=0, tiled=True, axis_index_groups=alike)  248 us
    reduce_scatter x3, waiting for transfers between devices, on_device(): lax.psum_scatter(both, 'lat', scatter_dimension=0, tiled=True, axis_index...  203 us
    pallas_call x3, Pallas kernels, dec_update(): pl.pallas_call(dec_kernel, grid=(width // block,), in_specs=whole + cols...  42.8 us
    ppermute x4, waiting for transfers between devices, across(): total = total + lax.ppermute(low, 'wid', ring).astype(jnp.float32)  33.9 us
    dot_general x6, matrix products, on_device(): lax.dot_general(errs[k][half], dec_half[k], (((1,), (1,)), ((), ())), pre...  23.7 us
    ppermute x7, waiting for transfers between devices, swap(): return lax.ppermute(x, 'lat', partner)  17 us
    dot_general x3, matrix products, on_device(): mine = jnp.dot(acts[0], dec_half[k], preferred_element_type=jnp.float32)  13.7 us
    pallas_call x1, Pallas kernels, enc_update(): pl.pallas_call(enc_kernel, grid=(width // block,), in_specs=cols + whole...  13.4 us
  transfers between devices with their start and end apart: 18, of which 12 were waited for; matrix products, arithmetic and copies ran while one was open for 8% of the time, Pallas kernels for 7%

profile of v1, /device:TPU:0, one launch (start us, length us, event | category | flops | bytes accessed | tf_op | source)
XLA Modules:
  0.0 656.9 jit_solution(4943375476675448686)
XLA Ops:
  9.1 65.1 %all-gather.5.cloned.1.call-done.src_a = bf16[896,1792]{1,0:T(8,128)(2,1)} async-done(((bf16[112,1792]{1,0:T(8,128)(2,1)}), bf16[896,1792]{1,0:T(8,128)(2,1)}) %all-gather.5.cloned.1.call-update) | async-done | bytes 3211280 | tf_op jit(solution)/shard_map/all_gather | solution.py:111
  74.2 6.8 %fusion.25 = (bf16[896,512]{0,1:T(8,128)(2,1)}, f32[896,512]{0,1:T(8,128)}) fusion(bf16[896,1792]{1,0:T(8,128)(2,1)} %all-gather.5.cloned.1.call-done.src_a, f32[1792,512]{1,0:T(8,128)} %w_ref.4), kind=kOutput, calls=%fused_computation.53 | convolution fusion | flops 1645543424 | bytes 9633792 | tf_op jit(solution)/shard_map/dot_general | solution.py:124
  82.4 3.7 fusion.26
  86.7 3.0 convert.8
  89.6 14.7 %collective-permute-done.1 = bf16[896,512]{0,1:T(8,128)(2,1)S(1)} collective-permute-done((bf16[896,512]{0,1:T(8,128)(2,1)}, bf16[896,512]{0,1:T(8,128)(2,1)S(1)}, u32[]{:S(2)}, u32[]{:S(2)}) %collective-permute-start.1) | collective-permute-done | bytes 917536 | tf_op jit(solution)/shard_map/ppermute | solution.py:107
  104.4 19.2 %collective-permute-done.2 = bf16[896,512]{0,1:T(8,128)(2,1)S(1)} collective-permute-done((bf16[896,512]{0,1:T(8,128)(2,1)}, bf16[896,512]{0,1:T(8,128)(2,1)S(1)}, u32[]{:S(2)}, u32[]{:S(2)}) %collective-permute-start.2) | collective-permute-done | bytes 917536 | tf_op jit(solution)/shard_map/ppermute | solution.py:107
  124.5 5.6 fusion.1
  132.1 5.7 collective-permute-done.3
  137.8 3.6 add_convert_fusion.2
  141.6 3.4 convolution_convert_fusion.1
  145.2 5.6 collective-permute-done.4
  150.8 5.1 add_convert_fusion.1
  156.0 3.4 convolution_convert_fusion
  159.6 5.6 collective-permute-done.5
  165.2 5.1 add_convert_fusion
  171.3 44.8 %reduce-scatter.4.cloned.1.call-done = bf16[112,1792]{1,0:T(8,128)(2,1)} async-done(((bf16[896,1792]{1,0:T(8,128)(2,1)}), bf16[112,1792]{1,0:T(8,128)(2,1)}) %reduce-scatter.4.cloned.1.call-update) | async-done | bytes 401424 | tf_op jit(solution)/shard_map/reduce_scatter | solution.py:134
  216.1 79.1 %reduce-scatter.6.cloned.1.call-done = bf16[112,1792]{1,0:T(8,128)(2,1)} async-done(((bf16[896,1792]{1,0:T(8,128)(2,1)}), bf16[112,1792]{1,0:T(8,128)(2,1)}) %reduce-scatter.6.cloned.1.call-update) | async-done | bytes 401424 | tf_op jit(solution)/shard_map/reduce_scatter | solution.py:134
  295.2 78.9 %reduce-scatter.8.cloned.1.call-done = bf16[112,1792]{1,0:T(8,128)(2,1)} async-done(((bf16[896,1792]{1,0:T(8,128)(2,1)}), bf16[112,1792]{1,0:T(8,128)(2,1)}) %reduce-scatter.8.cloned.1.call-update) | async-done | bytes 401424 | tf_op jit(solution)/shard_map/reduce_scatter | solution.py:134
  378.1 58.5 %all-gather.7.cloned.1.call-done.err_a = bf16[896,1792]{1,0:T(8,128)(2,1)} async-done(((bf16[112,1792]{1,0:T(8,128)(2,1)}), bf16[896,1792]{1,0:T(8,128)(2,1)}) %all-gather.7.cloned.1.call-update) | async-done | bytes 3211280 | tf_op jit(solution)/shard_map/all_gather | solution.py:111
  436.6 62.0 %all-gather.9.cloned.1.call-done.err_a = bf16[896,1792]{1,0:T(8,128)(2,1)} async-done(((bf16[112,1792]{1,0:T(8,128)(2,1)}), bf16[896,1792]{1,0:T(8,128)(2,1)}) %all-gather.9.cloned.1.call-update) | async-done | bytes 3211280 | tf_op jit(solution)/shard_map/all_gather | solution.py:111
  498.6 62.1 %all-gather.11.cloned.1.call-done.err_a = bf16[896,1792]{1,0:T(8,128)(2,1)} async-done(((bf16[112,1792]{1,0:T(8,128)(2,1)}), bf16[896,1792]{1,0:T(8,128)(2,1)}) %all-gather.11.cloned.1.call-update) | async-done | bytes 3211280 | tf_op jit(solution)/shard_map/all_gather | solution.py:111
  560.7 4.7 fusion.5
  565.4 3.7 fusion.8
  569.2 3.6 fusion.28
  574.3 4.0 fusion.4
  578.3 4.0 fusion.7
  582.4 3.6 fusion.27
  586.5 14.0 %dec_update.3 = (f32[3,512,1792]{2,1,0:T(8,128)}, f32[3,512,1792]{2,1,0:T(8,128)}, f32[3,512,1792]{2,1,0:T(8,128)}) custom-call(bf16[512,896]{1,0:T(8,128)(2,1)S(1)} %bitcast.61, bf16[512,896]{1,0:T(8,128)(2,1)S(1)} %bitcast.64, bf16[896,1792]{1,0:T(8,128)(2,1)S(1)} %copy-done.1, bf16[896,1792]{1,0:T(8,128)(2,1)} %collective-permute-done.7.err_b, ...), custom_call_target="tpu_custom_call" | custom-call | flops 3288334336 | bytes 28442624 | tf_op jit(solution)/shard_map/dec_update/pallas_call | solution.py:45
  600.6 13.8 %dec_update.4 = (f32[3,512,1792]{2,1,0:T(8,128)}, f32[3,512,1792]{2,1,0:T(8,128)}, f32[3,512,1792]{2,1,0:T(8,128)}) custom-call(bf16[512,896]{1,0:T(8,128)(2,1)S(1)} %bitcast.62, bf16[512,896]{1,0:T(8,128)(2,1)S(1)} %bitcast.65, bf16[896,1792]{1,0:T(8,128)(2,1)S(1)} %copy-done.3, ...), custom_call_target="tpu_custom_call", output_to_operand_aliasing={{0}: (7, {}), {1}: (8, {}), {2}: (9, {})} | custom-call | flops 3288334336 | bytes 28442624 | tf_op jit(solution)/shard_map/dec_update/pallas_call | solution.py:45
  614.4 15.0 %dec_update.5 = (f32[3,512,1792]{2,1,0:T(8,128)}, f32[3,512,1792]{2,1,0:T(8,128)}, f32[3,512,1792]{2,1,0:T(8,128)}) custom-call(bf16[512,896]{1,0:T(8,128)(2,1)S(1)} %bitcast.63, bf16[512,896]{1,0:T(8,128)(2,1)S(1)} %bitcast.66, bf16[896,1792]{1,0:T(8,128)(2,1)S(1)} %copy-done.2, ...), custom_call_target="tpu_custom_call", output_to_operand_aliasing={{0}: (7, {}), {1}: (8, {}), {2}: (9, {})} | custom-call | flops 3288334336 | bytes 28442624 | tf_op jit(solution)/shard_map/dec_update/pallas_call | solution.py:45
  630.7 2.9 multiply_convert_fusion
  636.6 13.4 %enc_update.1 = (f32[1792,512]{1,0:T(8,128)}, f32[1792,512]{1,0:T(8,128)}, f32[1792,512]{1,0:T(8,128)}) custom-call(bf16[896,1792]{1,0:T(8,128)(2,1)S(1)} %copy-done, bf16[896,1792]{1,0:T(8,128)(2,1)} %copy-done.12, bf16[896,512]{1,0:T(8,128)(2,1)S(1)} %copy.45.gp_a, bf16[896,512]{1,0:T(8,128)(2,1)S(1)} %copy.46.gp_b, f32[1792,512]{1,0:T(8,128)} %w_ref.4, ...), custom_call_target="tpu_custom_call" | custom-call | tf_op jit(solution)/shard_map/enc_update/pallas_call | solution.py:73
  (96 shorter events, 18.6 us)
Async XLA Ops:
  7.2 67.0 %all-gather.5.cloned.1.call-start = ((), (), s32[]{:S(2)}) async-start(), calls=%async_computation.3 | async-start | bytes 3612672 | tf_op jit(solution)/shard_map/all_gather | solution.py:111
  9.0 207.1 %reduce-scatter.4.cloned.1.call-start = ((), (), s32[]{:S(2)}) async-start(), calls=%async_computation.4 | async-start | bytes 3612672 | tf_op jit(solution)/shard_map/reduce_scatter | solution.py:134
  74.1 8.3 %copy-start.7 = (f32[1792,512]{1,0:T(8,128)S(1)}, f32[1792,512]{1,0:T(8,128)}, u32[]{:S(2)}) copy-start(f32[1792,512]{1,0:T(8,128)} %w_ref.4) | copy-start | bytes 11010052
  74.2 8.3 %collective-permute-start = (bf16[896,1792]{1,0:T(8,128)(2,1)}, bf16[896,1792]{1,0:T(8,128)(2,1)S(1)}, u32[]{:S(2)}, u32[]{:S(2)}) collective-permute-start(bf16[896,1792]{1,0:T(8,128)(2,1)} %all-gather.5.cloned.1.call-done.src_a), channel_id=1, source_target_pairs={{0,2},{2,0},{4,6},{6,4},{8,10},{10,8},{12,14},{14,12},{16,18},{18,... | collective-permute-start | bytes 9633800 | tf_op jit(solution)/shard_map/ppermute | solution.py:100
  74.2 12.5 %slice-start = ((s8[11010048]{0:T(1024)(128)(4,1)}), s8[4194304]{0:T(1024)(128)(4,1)S(1)}, s32[]{:S(2)}) async-start(s8[11010048]{0:T(1024)(128)(4,1)} %bitcast.67), calls=%async_computation.10 | async-start | bytes 8388608
  74.2 12.5 %slice-start.1 = ((s8[11010048]{0:T(1024)(128)(4,1)}), s8[4194304]{0:T(1024)(128)(4,1)S(1)}, s32[]{:S(2)}) async-start(s8[11010048]{0:T(1024)(128)(4,1)} %bitcast.67), calls=%async_computation.11 | async-start | bytes 8388608
  80.9 5.7 slice-start.2
  80.9 23.4 %collective-permute-start.1 = (bf16[896,512]{0,1:T(8,128)(2,1)}, bf16[896,512]{0,1:T(8,128)(2,1)S(1)}, u32[]{:S(2)}, u32[]{:S(2)}) collective-permute-start(bf16[896,512]{0,1:T(8,128)(2,1)} %get-tuple-element.40), channel_id=1, source_target_pairs={{0,1},{1,0},{2,3},{3,2},{4,5},{5,4},{6,7},{7,6},{8,9},{9,8},{10,11... | collective-permute-start | bytes 2752520 | tf_op jit(solution)/shard_map/ppermute | solution.py:107
  86.1 38.4 %copy-start.21 = (f32[512]{0:T(512)S(1)}, f32[512]{0:T(512)}, u32[]{:S(2)}) copy-start(f32[512]{0:T(512)} %param.15) | copy-start | bytes 6148
  86.1 37.5 %collective-permute-start.2 = (bf16[896,512]{0,1:T(8,128)(2,1)}, bf16[896,512]{0,1:T(8,128)(2,1)S(1)}, u32[]{:S(2)}, u32[]{:S(2)}) collective-permute-start(bf16[896,512]{0,1:T(8,128)(2,1)} %get-tuple-element.42), channel_id=1, source_target_pairs={{0,1},{1,0},{2,3},{3,2},{4,5},{5,4},{6,7},{7,6},{8,9},{9,8},{10,11... | collective-permute-start | bytes 2752520 | tf_op jit(solution)/shard_map/ppermute | solution.py:107
  104.4 19.2 %copy-start.8 = (bf16[896,512]{0,1:T(8,128)(2,1)}, bf16[896,512]{0,1:T(8,128)(2,1)S(1)}, u32[]{:S(2)}) copy-start(bf16[896,512]{0,1:T(8,128)(2,1)S(1)} %collective-permute-done.1) | copy-start | bytes 2752516
  132.0 5.8 collective-permute-start.3
  141.4 153.8 %reduce-scatter.6.cloned.1.call-start = ((), (), s32[]{:S(2)}) async-start(), calls=%async_computation.6 | async-start | bytes 3612672 | tf_op jit(solution)/shard_map/reduce_scatter | solution.py:134
  145.0 5.8 collective-permute-start.4
  155.9 218.3 %reduce-scatter.8.cloned.1.call-start = ((), (), s32[]{:S(2)}) async-start(), calls=%async_computation.8 | async-start | bytes 3612672 | tf_op jit(solution)/shard_map/reduce_scatter | solution.py:134
  159.3 5.8 collective-permute-start.5
  170.3 203.9 %copy-start.16 = (bf16[108,3,1792]{2,0,1:T(8,128)(2,1)S(1)}, bf16[108,3,1792]{2,0,1:T(8,128)(2,1)}, u32[]{:S(2)}) copy-start(bf16[108,3,1792]{2,0,1:T(8,128)(2,1)} %param.12) | copy-start | bytes 3483652
  170.3 266.3 %all-gather.7.cloned.1.call-start = ((), (), s32[]{:S(2)}) async-start(), calls=%async_computation.5 | async-start | bytes 3612672 | tf_op jit(solution)/shard_map/all_gather | solution.py:111
  376.8 121.8 %all-gather.9.cloned.1.call-start = ((), (), s32[]{:S(2)}) async-start(), calls=%async_computation.7 | async-start | bytes 3612672 | tf_op jit(solution)/shard_map/all_gather | solution.py:111
  377.4 183.3 %all-gather.11.cloned.1.call-start = ((), (), s32[]{:S(2)}) async-start(), calls=%async_computation.9 | async-start | bytes 3612672 | tf_op jit(solution)/shard_map/all_gather | solution.py:111
  436.6 137.8 %collective-permute-start.7 = (bf16[896,1792]{1,0:T(8,128)(2,1)}, bf16[896,1792]{1,0:T(8,128)(2,1)}, u32[]{:S(2)}, u32[]{:S(2)}) collective-permute-start(bf16[896,1792]{1,0:T(8,128)(2,1)} %all-gather.7.cloned.1.call-done.err_a), channel_id=1, source_target_pairs={{0,2},{2,0},{4,6},{6,4},{8,10},{10,8},{12,14},{14,12},{16,18},{18,... | collective-permute-start | bytes 9633800 | tf_op jit(solution)/shard_map/ppermute | solution.py:100
  498.5 79.8 %collective-permute-start.8 = (bf16[896,1792]{1,0:T(8,128)(2,1)}, bf16[896,1792]{1,0:T(8,128)(2,1)}, u32[]{:S(2)}, u32[]{:S(2)}) collective-permute-start(bf16[896,1792]{1,0:T(8,128)(2,1)} %all-gather.9.cloned.1.call-done.err_a), channel_id=1, source_target_pairs={{0,2},{2,0},{4,6},{6,4},{8,10},{10,8},{12,14},{14,12},{16,18},{18,... | collective-permute-start | bytes 9633800 | tf_op jit(solution)/shard_map/ppermute | solution.py:100
  560.7 21.7 %collective-permute-start.9 = (bf16[896,1792]{1,0:T(8,128)(2,1)}, bf16[896,1792]{1,0:T(8,128)(2,1)S(1)}, u32[]{:S(2)}, u32[]{:S(2)}) collective-permute-start(bf16[896,1792]{1,0:T(8,128)(2,1)} %all-gather.11.cloned.1.call-done.err_a), channel_id=1, source_target_pairs={{0,2},{2,0},{4,6},{6,4},{8,10},{10,8},{12,14},{14,12},{16,18},{18,... | collective-permute-start | bytes 9633800 | tf_op jit(solution)/shard_map/ppermute | solution.py:100
  560.7 8.5 %slice-start.3 = ((s8[5505024]{0:T(1024)(128)(4,1)}), s8[4194304]{0:T(1024)(128)(4,1)S(1)}, s32[]{:S(2)}) async-start(s8[5505024]{0:T(1024)(128)(4,1)} %bitcast.69), calls=%async_computation.13 | async-start | bytes 8388608
  572.8 56.6 %collective-permute-start.6 = (bf16[896,512]{0,1:T(8,128)(2,1)}, bf16[896,512]{0,1:T(8,128)(2,1)S(1)}, u32[]{:S(2)}, u32[]{:S(2)}) collective-permute-start(bf16[896,512]{0,1:T(8,128)(2,1)} %get-tuple-element.46), channel_id=1, source_target_pairs={{0,1},{1,0},{2,3},{3,2},{4,5},{5,4},{6,7},{7,6},{8,9},{9,8},{10,11... | collective-permute-start | bytes 2752520 | tf_op jit(solution)/shard_map/ppermute | solution.py:107
  586.0 43.4 %collective-permute-start.10 = (bf16[896,512]{0,1:T(8,128)(2,1)}, bf16[896,512]{0,1:T(8,128)(2,1)S(1)}, u32[]{:S(2)}, u32[]{:S(2)}) collective-permute-start(bf16[896,512]{0,1:T(8,128)(2,1)} %get-tuple-element.44), channel_id=1, source_target_pairs={{0,1},{1,0},{2,3},{3,2},{4,5},{5,4},{6,7},{7,6},{8,9},{9,8},{10,11... | collective-permute-start | bytes 2752520 | tf_op jit(solution)/shard_map/ppermute | solution.py:107
  614.3 16.3 %copy-start.4 = (f32[896,512]{0,1:T(8,128)S(1)}, f32[896,512]{0,1:T(8,128)}, u32[]{:S(2)}) copy-start(f32[896,512]{0,1:T(8,128)} %get-tuple-element.41) | copy-start | bytes 5505028
  614.3 16.3 %copy-start.5 = (f32[896,512]{0,1:T(8,128)S(1)}, f32[896,512]{0,1:T(8,128)}, u32[]{:S(2)}) copy-start(f32[896,512]{0,1:T(8,128)} %get-tuple-element.43) | copy-start | bytes 5505028
  614.3 16.3 %copy-start.9 = (bf16[896,512]{0,1:T(8,128)(2,1)S(1)}, bf16[896,512]{0,1:T(8,128)(2,1)}, u32[]{:S(2)}) copy-start(bf16[896,512]{0,1:T(8,128)(2,1)} %copy-done.8) | copy-start | bytes 2752516
  614.3 16.3 %copy-start.11 = (bf16[896,512]{0,1:T(8,128)(2,1)S(1)}, bf16[896,512]{0,1:T(8,128)(2,1)}, u32[]{:S(2)}) copy-start(bf16[896,512]{0,1:T(8,128)(2,1)} %copy-done.10) | copy-start | bytes 2752516
  614.4 16.3 %copy-start.14 = (f32[896,512]{0,1:T(8,128)S(1)}, f32[896,512]{0,1:T(8,128)}, u32[]{:S(2)}) copy-start(f32[896,512]{0,1:T(8,128)} %get-tuple-element.47) | copy-start | bytes 5505028
  614.4 16.3 %copy-start.15 = (f32[896,512]{0,1:T(8,128)S(1)}, f32[896,512]{0,1:T(8,128)}, u32[]{:S(2)}) copy-start(f32[896,512]{0,1:T(8,128)} %get-tuple-element.45) | copy-start | bytes 5505028
  (13 other events, 36.1 us)
Sparse Core Ops, SparseCore 0:
  10.7 63.3 all-gather.4
  141.5 74.5 reduce-scatter.3
  220.3 74.9 reduce-scatter.5
  299.3 74.8 reduce-scatter.7
  376.9 59.6 all-gather.6
  439.2 59.3 all-gather.8
  501.3 59.3 all-gather.10
